TPU v7x, 128 devices: a whole 4x4x4 slice. The times are simulated.
128 devices in a mesh: ent: 32 (over x_hi, z, y), sec: 4 (over x_lo, core).
Axes of the slice: x: 4 (x_hi: 2, x_lo: 2; x = x_hi * 2 + x_lo), y: 4, z: 4, core: 2. Of those that a mesh axis runs over, the one named last changes fastest.
Arguments:
- features: bfloat16 [4096, 256], P('ent'), may hold values from -6 to 6
- theta: bfloat16 [256, 256], replicated, may hold values from -3 to 3
- section_weight: float32 [65536], P(('ent', 'sec')), may hold values from 0.5 to 2
- pair_rows: int32 [128, 32, 512], P(('ent', 'sec')), may hold values from 0 to 511
- pair_cols: int32 [128, 32, 512], P(('ent', 'sec')), may hold values from 0 to 127
- pair_counts: int32 [128, 32], P(('ent', 'sec')), may hold values from 0 to 512, as said below
- cotangent: bfloat16 [4096, 256], P('ent'), may hold values from -24 to 24
Outputs:
- activated: bfloat16 [4096, 256], P('ent')
- grad_features: bfloat16 [4096, 256], P('ent')
- grad_theta: float32 [256, 256], replicated
- grad_weight: float32 [65536], P(('ent', 'sec'))
Inputs may be any that keep to these rules, and one draw needn't show every extreme that they name: Only the first pair_counts[k, j] slots of shard k and block j are used; some shard uses all 512 slots of some block.
All inputs are finite; a program needn't handle non-finite values.
Results may differ from a plain program's by a relative error of at most 0.0059.
Values may be sent and summed in bfloat16 or wider, within the bound.
A program may use at most 64 MiB of HBM per device.

v0:
```python
import jax
import jax.numpy as jnp
from jax import lax
from jax.sharding import PartitionSpec as P


def hot_table(indices, live_slots, offset, table_width):
    hits = (indices - offset)[:, None] == jnp.arange(table_width, dtype=jnp.int32)[None, :]
    return (hits & live_slots[:, None]).astype(jnp.bfloat16)


def body(features, theta, section_weight, pair_rows, pair_cols, pair_counts, cotangent):
    ent_dev = features.shape[0]
    feature_width = features.shape[1]
    sec_dev = section_weight.shape[0]
    blocks_count = pair_rows.shape[1]
    slot_count = pair_rows.shape[2]
    own_block = lax.axis_index("ent")
    row_lists = pair_rows[0]
    col_lists = pair_cols[0]
    usable = jnp.arange(slot_count, dtype=jnp.int32)[None, :] < pair_counts[0][:, None]
    usable_float = usable.astype(jnp.float32)
    entity_index = jnp.arange(blocks_count, dtype=jnp.int32)[:, None] * ent_dev + col_lists
    local_degree = jax.ops.segment_sum(
        usable_float.reshape(-1), entity_index.reshape(-1), num_segments=blocks_count * ent_dev
    )
    entity_degree = lax.psum(local_degree, ("ent", "sec"))
    own_degree = lax.dynamic_slice_in_dim(entity_degree, own_block * ent_dev, ent_dev)
    entity_scale = lax.rsqrt(1.0 + own_degree)[:, None]
    sec_count = jax.ops.segment_sum(
        usable_float.reshape(-1), row_lists.reshape(-1), num_segments=sec_dev
    )
    section_scale = (section_weight / (1.0 + sec_count))[:, None]

    def entity_fold(running, incoming, start_row):
        row_count = incoming.shape[0]
        span_width = min(row_count, ent_dev)
        block_span = max(row_count // ent_dev, 1)
        offset = start_row

        def add_block(turn_index, accum):
            row_slots = lax.dynamic_index_in_dim(row_lists, turn_index, 0, keepdims=False)
            col_slots = lax.dynamic_index_in_dim(col_lists, turn_index, 0, keepdims=False)
            live_slots = lax.dynamic_index_in_dim(usable, turn_index, 0, keepdims=False)
            values = lax.dynamic_slice_in_dim(incoming, turn_index * span_width, span_width, 0)
            col_hot = hot_table(col_slots, live_slots, offset, span_width)
            row_hot = hot_table(row_slots, live_slots, 0, sec_dev)
            picked = jnp.dot(col_hot, values, preferred_element_type=jnp.float32).astype(
                jnp.bfloat16
            )
            return accum + jnp.einsum(
                "ps,pf->sf", row_hot, picked, preferred_element_type=jnp.float32
            )

        return lax.fori_loop(0, block_span, add_block, running)

    def entity_terms(messages, start_row):
        span_width = min(lax.axis_size("ent") * ent_dev, ent_dev)
        block_span = max(lax.axis_size("ent") * ent_dev // ent_dev, 1)
        offset = start_row

        def block_term(turn_index):
            row_slots = lax.dynamic_index_in_dim(row_lists, turn_index, 0, keepdims=False)
            col_slots = lax.dynamic_index_in_dim(col_lists, turn_index, 0, keepdims=False)
            live_slots = lax.dynamic_index_in_dim(usable, turn_index, 0, keepdims=False)
            row_hot = hot_table(row_slots, live_slots, 0, sec_dev)
            col_hot = hot_table(col_slots, live_slots, offset, span_width)
            picked = jnp.dot(row_hot, messages, preferred_element_type=jnp.float32).astype(
                jnp.bfloat16
            )
            return jnp.einsum("pw,pf->wf", col_hot, picked, preferred_element_type=jnp.float32)

        pieces = lax.map(block_term, jnp.arange(block_span, dtype=jnp.int32))
        return pieces.reshape(block_span * span_width, feature_width)

    def collect(messages):
        partial_sum = lax.psum_scatter(
            entity_terms(messages, jnp.int32(0)), "ent", scatter_dimension=0, tiled=True
        )
        return lax.psum(partial_sum, "sec")

    zero_sections = jnp.zeros((sec_dev, feature_width), jnp.float32)
    projected = jnp.dot(features, theta, preferred_element_type=jnp.float32)
    scaled = (entity_scale * projected).astype(jnp.bfloat16)
    gathered = entity_fold(
        zero_sections, lax.all_gather(scaled, "ent", axis=0, tiled=True), jnp.int32(0)
    )
    messages = (section_scale * gathered).astype(jnp.bfloat16)
    collected = collect(messages)
    preact = entity_scale * collected
    activated = jax.nn.silu(preact).astype(jnp.bfloat16)
    sigmoid_pre = jax.nn.sigmoid(preact)
    grad_pre = cotangent.astype(jnp.float32) * sigmoid_pre * (1.0 + preact * (1.0 - sigmoid_pre))
    back_scaled = (entity_scale * grad_pre).astype(jnp.bfloat16)
    back_gathered = entity_fold(
        zero_sections, lax.all_gather(back_scaled, "ent", axis=0, tiled=True), jnp.int32(0)
    )
    grad_weight = jnp.sum(gathered * back_gathered, axis=1) / (1.0 + sec_count)
    back_messages = (section_scale * back_gathered).astype(jnp.bfloat16)
    back_collected = collect(back_messages)
    grad_proj = (entity_scale * back_collected).astype(jnp.bfloat16)
    grad_features = lax.dot_general(
        grad_proj, theta, (((1,), (1,)), ((), ())), preferred_element_type=jnp.float32
    ).astype(jnp.bfloat16)
    local_theta = lax.dot_general(
        features, grad_proj, (((0,), (0,)), ((), ())), preferred_element_type=jnp.float32
    )
    grad_theta = lax.psum(local_theta, "ent")
    return (activated, grad_features, grad_theta, grad_weight)


def solution(mesh):
    placed = (
        P("ent", None),
        P(),
        P(("ent", "sec")),
        P(("ent", "sec"), None, None),
        P(("ent", "sec"), None, None),
        P(("ent", "sec"), None),
        P("ent", None),
    )
    return jax.shard_map(
        body,
        mesh=mesh,
        in_specs=placed,
        out_specs=(P("ent", None), P("ent", None), P(), P(("ent", "sec"))),
        check_vma=False,
    )
```

profile of v0, /device:TPU:0, one launch (start us, length us, event | category | flops | bytes accessed | tf_op | source)
XLA Modules:
  0.0 1644.0 jit_solution(5554662827985014451)
XLA Ops:
  9.2 113.5 %scatter_custom_fusion = f32[4096]{0:T(1024)S(1)} fusion(s32[16384]{0:T(1024)S(1)} %bitcast.81, f32[16384]{0:T(1024)S(1)} %bitcast.82, f32[]{:T(128)} %constant.131.clone.1), kind=kCustom, calls=%fused_computation.76 | custom fusion | flops 16384 | bytes 16388 | tf_op jit(solution)/shard_map/scatter-add | solution.py:24
  122.6 68.3 %psum.28 = f32[4096]{0:T(1024)S(1)} all-reduce(f32[4096]{0:T(1024)S(1)} %scatter_custom_fusion), channel_id=1, replica_groups=mesh['ent'=32,'sec'=4] {'ent','sec'}, use_global_device_ids=true, to_apply=%region_1.0 | all-reduce | flops 4096 | bytes 32768 | tf_op jit(solution)/shard_map/psum | solution.py:27
  193.5 113.4 %scatter_custom_fusion.1 = f32[512]{0:T(512)S(1)} fusion(s32[16384]{0:T(1024)S(1)} %bitcast.84, f32[16384]{0:T(1024)S(1)} %bitcast.83, f32[]{:T(128)} %constant.137.clone.1), kind=kCustom, calls=%fused_computation.78 | custom fusion | flops 16384 | bytes 2052 | tf_op jit(solution)/shard_map/scatter-add | solution.py:30
  307.7 79.9 %while.50 = (s32[]{:T(128)}, f32[512,256]{1,0:T(8,128)S(1)}, s32[32,512]{1,0:T(8,128)}, pred[32,512]{1,0:T(8,128)(4,1)S(1)}, s32[32,512]{1,0:T(8,128)}, /*index=...) while((s32[]{:T(128)}, f32[512,256]{1,0:T(8,128)S(1)}, ...), condition=%wide.region_4.5_spmd.clone, body=%wide.region_3.4_spmd.clone.sunk | while | flops 168820736 | bytes 1128617 | solution.py:55
  313.4 1.7 convolution_add_fusion.4
  315.9 1.7 convolution_add_fusion.4
  330.9 1.7 convolution_add_fusion.4
  333.4 1.7 convolution_add_fusion.4
  348.4 1.7 convolution_add_fusion.4
  350.9 1.7 convolution_add_fusion.4
  365.9 1.7 convolution_add_fusion.4
  368.4 1.7 convolution_add_fusion.4
  383.4 1.7 convolution_add_fusion.4
  385.9 1.7 convolution_add_fusion.4
  387.7 2.4 broadcast.21.clone
  390.2 144.5 %while.48 = (s32[]{:T(128)}, f32[32,128,256]{2,1,0:T(8,128)}, s32[32]{0:T(128)S(1)}, s32[32,512]{1,0:T(8,128)}, pred[32,512]{1,0:T(8,128)(4,1)S(1)}, /*index=5*/...) while((s32[]{:T(128)}, f32[32,128,256]{2,1,0:T(8,128)}, ...), condition=%wide.region_6.7_spmd, body=%wide.region_5.6_spmd.sunk | while | flops 168558592 | bytes 408219 | solution.py:73
  534.8 188.6 %reduce-scatter.3.cloned.1.call-done = f32[128,256]{1,0:T(8,128)} async-done(((f32[4096,256]{1,0:T(8,128)}), f32[128,256]{1,0:T(8,128)}) %reduce-scatter.3.cloned.1.call-update) | async-done | bytes 131088 | tf_op jit(solution)/shard_map/reduce_scatter | solution.py:77
  723.4 32.8 %all-reduce.4.cloned.1.call-done = f32[128,256]{1,0:T(8,128)} async-done(((f32[128,256]{1,0:T(8,128)}), f32[128,256]{1,0:T(8,128)}) %all-reduce.4.cloned.1.call-update) | async-done | bytes 131088 | tf_op jit(solution)/shard_map/psum | solution.py:80
  756.2 1.7 multiply_convert_fusion.3
  758.0 73.9 %all-gather.5.cloned.1.call-done = bf16[4096,256]{1,0:T(8,128)(2,1)} async-done(((bf16[128,256]{1,0:T(8,128)(2,1)}), bf16[4096,256]{1,0:T(8,128)(2,1)}) %all-gather.5.cloned.1.call-update) | async-done | bytes 2097168 | tf_op jit(solution)/shard_map/all_gather | solution.py:96
  831.9 79.9 %while.51 = (s32[]{:T(128)}, f32[512,256]{1,0:T(8,128)S(1)}, s32[32,512]{1,0:T(8,128)}, pred[32,512]{1,0:T(8,128)(4,1)S(1)}, s32[32,512]{1,0:T(8,128)}, /*index=...) while((s32[]{:T(128)}, f32[512,256]{1,0:T(8,128)S(1)}, ...), condition=%wide.region_10.11_spmd.clone, body=%wide.region_9.10_spmd.clone.sunk | while | flops 168820736 | bytes 1128617 | solution.py:55
  832.6 1.7 convolution_add_fusion.5
  842.6 1.7 convolution_add_fusion.5
  845.1 1.7 convolution_add_fusion.5
  912.0 2.4 broadcast.21
  914.4 144.5 %while.49 = (s32[]{:T(128)}, f32[32,128,256]{2,1,0:T(8,128)}, s32[32]{0:T(128)S(1)}, s32[32,512]{1,0:T(8,128)}, pred[32,512]{1,0:T(8,128)(4,1)S(1)}, /*index=5*/...) while((s32[]{:T(128)}, f32[32,128,256]{2,1,0:T(8,128)}, ...), condition=%wide.region_12.13_spmd, body=%wide.region_11.12_spmd.sunk | while | flops 168558592 | bytes 408219 | solution.py:73
  1059.0 190.6 %reduce-scatter.5.cloned.1.call-done = f32[128,256]{1,0:T(8,128)} async-done(((f32[4096,256]{1,0:T(8,128)}), f32[128,256]{1,0:T(8,128)}) %reduce-scatter.5.cloned.1.call-update) | async-done | bytes 131088 | tf_op jit(solution)/shard_map/reduce_scatter | solution.py:77
  1249.7 32.8 %all-reduce.6.cloned.1.call-done = f32[128,256]{1,0:T(8,128)} async-done(((f32[128,256]{1,0:T(8,128)}), f32[128,256]{1,0:T(8,128)}) %all-reduce.6.cloned.1.call-update) | async-done | bytes 131088 | tf_op jit(solution)/shard_map/psum | solution.py:80
  1282.5 1.9 convolution_bitcast_fusion
  1285.0 1.7 convolution_convert_fusion.4
  1286.8 348.6 %all-reduce.8.cloned.1.call-done = f32[256,256]{0,1:T(8,128)} async-done(((f32[256,256]{0,1:T(8,128)}), f32[256,256]{0,1:T(8,128)}) %all-reduce.8.cloned.1.call-update) | async-done | bytes 262160 | tf_op jit(solution)/shard_map/psum | solution.py:108
  1635.4 1.8 copy.11
  (474 shorter events, 307.0 us)
Async XLA Ops:
  7.2 183.8 %copy-start = (bf16[256,256]{1,0:T(8,128)(2,1)S(1)}, bf16[256,256]{1,0:T(8,128)(2,1)}, u32[]{:S(2)}) copy-start(bf16[256,256]{1,0:T(8,128)(2,1)} %param.16) | copy-start | bytes 393220
  7.2 300.5 %all-gather.3.cloned.1.call-start = ((), (), s32[]{:S(2)}) async-start(), calls=%async_computation.2 | async-start | bytes 2162688 | tf_op jit(solution)/shard_map/all_gather | solution.py:86
  192.6 530.7 %reduce-scatter.3.cloned.1.call-start = ((), (), s32[]{:S(2)}) async-start(), calls=%async_computation.3 | async-start | bytes 4325376 | tf_op jit(solution)/shard_map/reduce_scatter | solution.py:77
  390.1 366.0 %copy-start.2 = (bf16[128,256]{1,0:T(8,128)(2,1)S(1)}, bf16[128,256]{1,0:T(8,128)(2,1)}, u32[]{:S(2)}) copy-start(bf16[128,256]{1,0:T(8,128)(2,1)} %param.21) | copy-start | bytes 196612
  534.7 221.5 %all-reduce.4.cloned.1.call-start = ((), (), s32[]{:S(2)}) async-start(), calls=%async_computation.4 | async-start | bytes 262144 | tf_op jit(solution)/shard_map/psum | solution.py:80
  723.4 108.5 %all-gather.5.cloned.1.call-start = ((), (), s32[]{:S(2)}) async-start(), calls=%async_computation.5 | async-start | bytes 2162688 | tf_op jit(solution)/shard_map/all_gather | solution.py:96
  757.9 491.7 %reduce-scatter.5.cloned.1.call-start = ((), (), s32[]{:S(2)}) async-start(), calls=%async_computation.6 | async-start | bytes 4325376 | tf_op jit(solution)/shard_map/reduce_scatter | solution.py:77
  914.4 368.1 %copy-start.1 = (bf16[128,256]{1,0:T(8,128)(2,1)S(1)}, bf16[128,256]{1,0:T(8,128)(2,1)}, u32[]{:S(2)}) copy-start(bf16[128,256]{1,0:T(8,128)(2,1)} %param.15) | copy-start | bytes 196612
  1059.0 223.6 %all-reduce.6.cloned.1.call-start = ((), (), s32[]{:S(2)}) async-start(), calls=%async_computation.7 | async-start | bytes 262144 | tf_op jit(solution)/shard_map/psum | solution.py:80
  1249.7 385.8 %all-reduce.8.cloned.1.call-start = ((), (), s32[]{:S(2)}) async-start(), calls=%async_computation.8 | async-start | bytes 524288 | tf_op jit(solution)/shard_map/psum | solution.py:108
Sparse Core Ops, SparseCore 0:
  192.7 66.8 all-gather.2
  534.8 188.4 reduce-scatter.2
  725.8 30.3 all-reduce.3
  760.1 71.6 all-gather.4
  1059.1 190.4 reduce-scatter.4
  1252.1 30.3 all-reduce.5
  1285.6 349.7 all-reduce.7
where the time goes:
time: 1670 us; the launch traced here: 1640 us
  waiting for transfers between devices  867 us (52%)
  other arithmetic  231 us (14%)
  matrix products  191 us (11%)
  local copies, waits for them, and re-layouts  145 us (9%)
  loops' own time  126 us (8%)
  blocking collectives  68.3 us (4%)
    reduce_scatter x2, waiting for transfers between devices, collect(): lax.psum_scatter(entity_terms(messages, jnp.int32(0)), 'ent', scatter_dim...  379 us
    psum x1, waiting for transfers between devices, body(): grad_theta = lax.psum(local_theta, 'ent')  349 us
    another operation x2, loops' own time, entity_terms(): pieces = lax.map(block_term, jnp.arange(block_span, dtype=jnp.int32))  125 us
    scatter-add x1, other arithmetic, body(): jax.ops.segment_sum(usable_float.reshape(-1), entity_index.reshape(-1), n...  113 us
    scatter-add x1, other arithmetic, body(): jax.ops.segment_sum(usable_float.reshape(-1), row_lists.reshape(-1), num_...  113 us
    dot_general x64, matrix products, add_block(): jnp.einsum('ps,pf->sf', row_hot, picked, preferred_element_type=jnp.float32)  108 us
    dot_general x64, matrix products, block_term(): jnp.einsum('pw,pf->wf', col_hot, picked, preferred_element_type=jnp.float32)  77.7 us
    all_gather x1, waiting for transfers between devices, body(): lax.all_gather(back_scaled, 'ent', axis=0, tiled=True)  73.9 us
  transfers between devices with their start and end apart: 7, of which 6 were waited for; matrix products, arithmetic and copies ran while one was open for 7% of the time, Pallas kernels for 0%

commit v1 on v0

--- a/solution.py
+++ b/solution.py
@@ -24,7 +24,7 @@
     local_degree = jax.ops.segment_sum(
         usable_float.reshape(-1), entity_index.reshape(-1), num_segments=blocks_count * ent_dev
     )
-    entity_degree = lax.psum(local_degree, ("ent", "sec"))
+    entity_degree = lax.psum(lax.psum(local_degree, "sec"), "ent")
     own_degree = lax.dynamic_slice_in_dim(entity_degree, own_block * ent_dev, ent_dev)
     entity_scale = lax.rsqrt(1.0 + own_degree)[:, None]
     sec_count = jax.ops.segment_sum(

time: 1670 us -> 1800 us (1.078)
  blocking collectives: 68.3 us -> 196 us
    psum x1 -> x2, blocking collectives: 68.3 us -> 196 us  [body(): entity_degree = lax.psum(lax.psum(local_degree, 'sec'), 'ent')]
where the time goes in v1:
time: 1800 us; the launch traced here: 1770 us
  waiting for transfers between devices  866 us (48%)
  other arithmetic  231 us (13%)
  blocking collectives  196 us (11%)
  matrix products  191 us (11%)
  local copies, waits for them, and re-layouts  145 us (8%)
  loops' own time  126 us (7%)
    reduce_scatter x2, waiting for transfers between devices, collect(): lax.psum_scatter(entity_terms(messages, jnp.int32(0)), 'ent', scatter_dim...  378 us
    psum x1, waiting for transfers between devices, body(): grad_theta = lax.psum(local_theta, 'ent')  349 us
    psum x2, blocking collectives, body(): entity_degree = lax.psum(lax.psum(local_degree, 'sec'), 'ent')  196 us
    another operation x2, loops' own time, entity_terms(): pieces = lax.map(block_term, jnp.arange(block_span, dtype=jnp.int32))  125 us
    scatter-add x1, other arithmetic, body(): jax.ops.segment_sum(usable_float.reshape(-1), entity_index.reshape(-1), n...  113 us
    scatter-add x1, other arithmetic, body(): jax.ops.segment_sum(usable_float.reshape(-1), row_lists.reshape(-1), num_...  113 us
    dot_general x64, matrix products, add_block(): jnp.einsum('ps,pf->sf', row_hot, picked, preferred_element_type=jnp.float32)  108 us
    dot_general x64, matrix products, block_term(): jnp.einsum('pw,pf->wf', col_hot, picked, preferred_element_type=jnp.float32)  77.7 us
  transfers between devices with their start and end apart: 7, of which 6 were waited for; matrix products, arithmetic and copies ran while one was open for 7% of the time, Pallas kernels for 0%

profile of v1, /device:TPU:0, one launch (start us, length us, event | category | flops | bytes accessed | tf_op | source)
XLA Modules:
  0.0 1770.3 jit_solution(5947568650046441263)
XLA Ops:
  9.2 113.5 %scatter_custom_fusion = f32[4096]{0:T(1024)S(1)} fusion(s32[16384]{0:T(1024)S(1)} %bitcast.81, f32[16384]{0:T(1024)S(1)} %bitcast.82, f32[]{:T(128)} %constant.131.clone.1), kind=kCustom, calls=%fused_computation.76 | custom fusion | flops 16384 | bytes 16388 | tf_op jit(solution)/shard_map/scatter-add | solution.py:24
  122.6 11.3 psum.35
  133.9 184.8 %psum.36 = f32[4096]{0:T(1024)S(1)} all-reduce(f32[4096]{0:T(1024)S(1)} %psum.35), channel_id=1, replica_groups=mesh['ent'=32,'sec'=4] {'ent'}, use_global_device_ids=true, to_apply=%region_2.0 | all-reduce | flops 4096 | bytes 32768 | tf_op jit(solution)/shard_map/psum | solution.py:27
  321.3 113.4 %scatter_custom_fusion.1 = f32[512]{0:T(512)S(1)} fusion(s32[16384]{0:T(1024)S(1)} %bitcast.84, f32[16384]{0:T(1024)S(1)} %bitcast.83, f32[]{:T(128)} %constant.137.clone.1), kind=kCustom, calls=%fused_computation.78 | custom fusion | flops 16384 | bytes 2052 | tf_op jit(solution)/shard_map/scatter-add | solution.py:30
  435.5 79.9 %while.50 = (s32[]{:T(128)}, f32[512,256]{1,0:T(8,128)S(1)}, s32[32,512]{1,0:T(8,128)}, pred[32,512]{1,0:T(8,128)(4,1)S(1)}, s32[32,512]{1,0:T(8,128)}, /*index=...) while((s32[]{:T(128)}, f32[512,256]{1,0:T(8,128)S(1)}, ...), condition=%wide.region_5.6_spmd.clone, body=%wide.region_4.5_spmd.clone.sunk | while | flops 168820736 | bytes 1128617 | solution.py:55
  446.2 1.7 convolution_add_fusion.4
  448.7 1.7 convolution_add_fusion.4
  463.7 1.7 convolution_add_fusion.4
  466.2 1.7 convolution_add_fusion.4
  481.2 1.7 convolution_add_fusion.4
  483.7 1.7 convolution_add_fusion.4
  498.7 1.7 convolution_add_fusion.4
  501.2 1.7 convolution_add_fusion.4
  515.5 2.4 broadcast.21.clone
  517.9 144.5 %while.48 = (s32[]{:T(128)}, f32[32,128,256]{2,1,0:T(8,128)}, s32[32]{0:T(128)S(1)}, s32[32,512]{1,0:T(8,128)}, pred[32,512]{1,0:T(8,128)(4,1)S(1)}, /*index=5*/...) while((s32[]{:T(128)}, f32[32,128,256]{2,1,0:T(8,128)}, ...), condition=%wide.region_7.8_spmd, body=%wide.region_6.7_spmd.sunk | while | flops 168558592 | bytes 408219 | solution.py:73
  662.6 186.8 %reduce-scatter.3.cloned.1.call-done = f32[128,256]{1,0:T(8,128)} async-done(((f32[4096,256]{1,0:T(8,128)}), f32[128,256]{1,0:T(8,128)}) %reduce-scatter.3.cloned.1.call-update) | async-done | bytes 131088 | tf_op jit(solution)/shard_map/reduce_scatter | solution.py:77
  849.5 32.8 %all-reduce.4.cloned.1.call-done = f32[128,256]{1,0:T(8,128)} async-done(((f32[128,256]{1,0:T(8,128)}), f32[128,256]{1,0:T(8,128)}) %all-reduce.4.cloned.1.call-update) | async-done | bytes 131088 | tf_op jit(solution)/shard_map/psum | solution.py:80
  882.2 1.7 multiply_convert_fusion.3
  884.0 73.9 %all-gather.5.cloned.1.call-done = bf16[4096,256]{1,0:T(8,128)(2,1)} async-done(((bf16[128,256]{1,0:T(8,128)(2,1)}), bf16[4096,256]{1,0:T(8,128)(2,1)}) %all-gather.5.cloned.1.call-update) | async-done | bytes 2097168 | tf_op jit(solution)/shard_map/all_gather | solution.py:96
  957.9 79.9 %while.51 = (s32[]{:T(128)}, f32[512,256]{1,0:T(8,128)S(1)}, s32[32,512]{1,0:T(8,128)}, pred[32,512]{1,0:T(8,128)(4,1)S(1)}, s32[32,512]{1,0:T(8,128)}, /*index=...) while((s32[]{:T(128)}, f32[512,256]{1,0:T(8,128)S(1)}, ...), condition=%wide.region_11.12_spmd.clone, body=%wide.region_10.11_spmd.clone.sunk | while | flops 168820736 | bytes 1128617 | solution.py:55
  971.2 1.7 convolution_add_fusion.5
  973.7 1.7 convolution_add_fusion.5
  988.7 1.7 convolution_add_fusion.5
  1008.6 1.7 convolution_add_fusion.5
  1038.1 2.4 broadcast.21
  1040.5 144.5 %while.49 = (s32[]{:T(128)}, f32[32,128,256]{2,1,0:T(8,128)}, s32[32]{0:T(128)S(1)}, s32[32,512]{1,0:T(8,128)}, pred[32,512]{1,0:T(8,128)(4,1)S(1)}, /*index=5*/...) while((s32[]{:T(128)}, f32[32,128,256]{2,1,0:T(8,128)}, ...), condition=%wide.region_13.14_spmd, body=%wide.region_12.13_spmd.sunk | while | flops 168558592 | bytes 408219 | solution.py:73
  1185.1 190.9 %reduce-scatter.5.cloned.1.call-done = f32[128,256]{1,0:T(8,128)} async-done(((f32[4096,256]{1,0:T(8,128)}), f32[128,256]{1,0:T(8,128)}) %reduce-scatter.5.cloned.1.call-update) | async-done | bytes 131088 | tf_op jit(solution)/shard_map/reduce_scatter | solution.py:77
  1376.1 32.7 %all-reduce.6.cloned.1.call-done = f32[128,256]{1,0:T(8,128)} async-done(((f32[128,256]{1,0:T(8,128)}), f32[128,256]{1,0:T(8,128)}) %all-reduce.6.cloned.1.call-update) | async-done | bytes 131088 | tf_op jit(solution)/shard_map/psum | solution.py:80
  1408.8 1.9 convolution_bitcast_fusion
  1411.3 1.7 convolution_convert_fusion.4
  1413.1 348.6 %all-reduce.8.cloned.1.call-done = f32[256,256]{0,1:T(8,128)} async-done(((f32[256,256]{0,1:T(8,128)}), f32[256,256]{0,1:T(8,128)}) %all-reduce.8.cloned.1.call-update) | async-done | bytes 262160 | tf_op jit(solution)/shard_map/psum | solution.py:108
  1761.7 1.8 copy.11
  (475 shorter events, 308.7 us)
Async XLA Ops:
  7.2 311.6 %copy-start = (bf16[256,256]{1,0:T(8,128)(2,1)S(1)}, bf16[256,256]{1,0:T(8,128)(2,1)}, u32[]{:S(2)}) copy-start(bf16[256,256]{1,0:T(8,128)(2,1)} %param.16) | copy-start | bytes 393220
  7.2 428.3 %all-gather.3.cloned.1.call-start = ((), (), s32[]{:S(2)}) async-start(), calls=%async_computation.2 | async-start | bytes 2162688 | tf_op jit(solution)/shard_map/all_gather | solution.py:86
  320.4 529.0 %reduce-scatter.3.cloned.1.call-start = ((), (), s32[]{:S(2)}) async-start(), calls=%async_computation.3 | async-start | bytes 4325376 | tf_op jit(solution)/shard_map/reduce_scatter | solution.py:77
  517.9 364.3 %copy-start.2 = (bf16[128,256]{1,0:T(8,128)(2,1)S(1)}, bf16[128,256]{1,0:T(8,128)(2,1)}, u32[]{:S(2)}) copy-start(bf16[128,256]{1,0:T(8,128)(2,1)} %param.21) | copy-start | bytes 196612
  662.5 219.7 %all-reduce.4.cloned.1.call-start = ((), (), s32[]{:S(2)}) async-start(), calls=%async_computation.4 | async-start | bytes 262144 | tf_op jit(solution)/shard_map/psum | solution.py:80
  849.4 108.5 %all-gather.5.cloned.1.call-start = ((), (), s32[]{:S(2)}) async-start(), calls=%async_computation.5 | async-start | bytes 2162688 | tf_op jit(solution)/shard_map/all_gather | solution.py:96
  883.9 492.1 %reduce-scatter.5.cloned.1.call-start = ((), (), s32[]{:S(2)}) async-start(), calls=%async_computation.6 | async-start | bytes 4325376 | tf_op jit(solution)/shard_map/reduce_scatter | solution.py:77
  1040.5 368.3 %copy-start.1 = (bf16[128,256]{1,0:T(8,128)(2,1)S(1)}, bf16[128,256]{1,0:T(8,128)(2,1)}, u32[]{:S(2)}) copy-start(bf16[128,256]{1,0:T(8,128)(2,1)} %param.15) | copy-start | bytes 196612
  1185.0 223.8 %all-reduce.6.cloned.1.call-start = ((), (), s32[]{:S(2)}) async-start(), calls=%async_computation.7 | async-start | bytes 262144 | tf_op jit(solution)/shard_map/psum | solution.py:80
  1376.0 385.7 %all-reduce.8.cloned.1.call-start = ((), (), s32[]{:S(2)}) async-start(), calls=%async_computation.8 | async-start | bytes 524288 | tf_op jit(solution)/shard_map/psum | solution.py:108
Sparse Core Ops, SparseCore 0:
  320.5 64.8 all-gather.2
  662.6 186.7 reduce-scatter.2
  851.9 30.3 all-reduce.3
  886.2 71.6 all-gather.4
  1185.1 190.8 reduce-scatter.4
  1378.5 30.2 all-reduce.5
  1411.8 349.7 all-reduce.7
